TPU v7x, 32 devices: a whole 2x2x4 slice. The times are simulated.
32 devices in a mesh: cell: 2 (over y), gene: 16 (over z, x, core).
Axes of the slice: x: 2, y: 2, z: 4, core: 2. Of those that a mesh axis runs over, the one named last changes fastest.
Arguments:
- blocks: bfloat16 [1536, 256, 256], P(('cell', 'gene')), may hold values from 0 to 255, as said below
- block_rows: int32 [1536], P(('cell', 'gene')), may hold values from 0 to 15, as said below
- block_cols: int32 [1536], P(('cell', 'gene')), may hold values from 0 to 3, as said below
- block_count: int32 [32], P(('cell', 'gene')), may hold values from 2 to 48, as said below
- cell_factor: float32 [8192, 128], P(('cell', 'gene')), as said below
- gene_factor: float32 [16384, 128], P('gene'), as said below
Outputs:
- cell_new: float32 [8192, 128], P(('cell', 'gene'))
- gene_new: float32 [16384, 128], P('gene')
Inputs may be any that keep to these rules, and one draw needn't show every extreme that they name: `blocks`: counts are whole numbers. `block_rows`: within one device the live slots and the padding slots name distinct block positions. `block_cols`: within one device the live slots and the padding slots name distinct block positions. `block_count`: some device has all 48 slots live. `cell_factor`: positive entries. `gene_factor`: positive entries.
All inputs are finite; a program needn't handle non-finite values.
Results may differ from a plain program's by a relative error of at most 0.00084.
Values may be sent and summed in bfloat16 or wider, within the bound.
A program may use at most 64 MiB of HBM per device.

v0:
```python
import jax
import jax.numpy as jnp
from jax import lax
from jax.sharding import PartitionSpec as P


def block_ratio(blocks, row_tiles, col_tiles, live):
    model = jnp.einsum("nir,njr->nij", row_tiles, col_tiles, preferred_element_type=jnp.float32)
    return (blocks.astype(jnp.float32) / model * live[:, None, None]).astype(jnp.bfloat16)


def on_device(blocks, block_rows, block_cols, block_count, cell_factor, gene_factor):
    slots = blocks.shape[0]
    width = blocks.shape[1]
    rank = cell_factor.shape[1]
    gene_len = gene_factor.shape[0]
    live = (jnp.arange(slots, dtype=jnp.int32) < block_count[0]).astype(jnp.float32)
    gene_bf = gene_factor.astype(jnp.bfloat16)
    gene_tiles = gene_bf.reshape(-1, width, rank)[block_cols]
    gene_totals = lax.psum(jnp.sum(gene_factor, 0), "gene")
    cell_full = lax.all_gather(cell_factor, "gene", axis=0, tiled=True)
    cell_bf = cell_full.astype(jnp.bfloat16)
    row_count = cell_bf.shape[0] // width
    row_pick = (block_rows[None, :] == jnp.arange(row_count, dtype=jnp.int32)[:, None]).astype(
        jnp.float32
    )
    col_pick = (
        block_cols[None, :] == jnp.arange(gene_len // width, dtype=jnp.int32)[:, None]
    ).astype(jnp.float32)
    row_tiles = cell_bf.reshape(row_count, width, rank)[block_rows]
    ratio = block_ratio(blocks, row_tiles, gene_tiles, live)
    terms = jnp.einsum("nij,njr->nir", ratio, gene_tiles, preferred_element_type=jnp.float32)
    numer = jnp.einsum("bn,nir->bir", row_pick, terms, precision=lax.Precision.HIGHEST).reshape(
        -1, rank
    )
    whole = lax.psum(numer, "gene")
    group_new = cell_full * whole / gene_totals
    new_bf = group_new.astype(jnp.bfloat16)
    cell_sums = lax.psum(jnp.sum(group_new, 0), "cell")
    own_rows = cell_factor.shape[0]
    cell_new = lax.dynamic_slice_in_dim(group_new, lax.axis_index("gene") * own_rows, own_rows, 0)
    new_tiles = new_bf.reshape(row_count, width, rank)[block_rows]
    ratio_next = block_ratio(blocks, new_tiles, gene_tiles, live)
    terms_next = jnp.einsum(
        "nij,nir->njr", ratio_next, new_tiles, preferred_element_type=jnp.float32
    )
    numer_gene = jnp.einsum(
        "bn,njr->bjr", col_pick, terms_next, precision=lax.Precision.HIGHEST
    ).reshape(-1, rank)
    total = lax.psum(numer_gene, "cell")
    gene_new = gene_factor * total / cell_sums
    return (cell_new, gene_new)


def solution(mesh):
    placed = (
        P(("cell", "gene"), None, None),
        P(("cell", "gene")),
        P(("cell", "gene")),
        P(("cell", "gene")),
        P(("cell", "gene"), None),
        P("gene", None),
    )
    return jax.shard_map(
        on_device,
        mesh=mesh,
        in_specs=placed,
        out_specs=(P(("cell", "gene"), None), P("gene", None)),
        check_vma=False,
    )
```

profile of v0, /device:TPU:0, one launch (start us, length us, event | category | flops | bytes accessed | tf_op | source)
XLA Modules:
  0.0 241.2 jit_solution(14404089688201856968)
XLA Ops:
  7.2 0.0 all-gather.2.cloned.1.call-start
  7.2 0.7 all-gather.2.cloned.1.call-update
  7.9 0.0 all-reduce.3.cloned.1.call-start
  8.6 0.7 compare_select_fusion
  9.3 1.4 fusion.23
  10.7 0.0 copy-start.1
  10.7 2.8 %gather_fusion.1 = bf16[48,256,128]{2,1,0:T(8,128)(2,1)} fusion(bf16[4,256,128]{2,1,0:T(8,128)(2,1)S(1)} %bitcast.19, s32[1024]{0:T(1024)S(1)} %pad_clamp_fusion), kind=kCustom, calls=%fused_computation.1 | custom fusion | bytes 6291648 | tf_op jit(solution)/shard_map/gather | solution.py:19
  13.4 0.0 copy-done.1
  13.5 40.9 %all-gather.2.cloned.1.call-done = f32[4096,128]{1,0:T(8,128)} async-done(((f32[256,128]{1,0:T(8,128)}), f32[4096,128]{1,0:T(8,128)}) %all-gather.2.cloned.1.call-update) | async-done | bytes 2097168 | tf_op jit(solution)/shard_map/all_gather | solution.py:21
  54.3 1.7 convert_element_type.29
  56.0 2.7 %gather_fusion = bf16[48,256,128]{2,1,0:T(8,128)(2,1)} fusion(bf16[16,256,128]{2,1,0:T(8,128)(2,1)S(1)} %bitcast.21, s32[1024]{0:T(1024)S(1)} %pad_clamp_fusion.1), kind=kCustom, calls=%fused_computation | custom fusion | bytes 6291648 | tf_op jit(solution)/shard_map/gather | solution.py:30
  58.7 11.7 %fusion.10 = f32[48,256,128]{2,1,0:T(8,128)} fusion(bf16[48,256,128]{2,1,0:T(8,128)(2,1)} %gather_fusion.1, bf16[48,256,256]{2,1,0:T(8,128)(2,1)} %param.6, f32[48]{0:T(128)S(1)} %compare_convert_fusion, bf16[48,256,128]{2,1,0:T(8,128)(2,1)} %gather_fusion), kind=kOutput, calls=%fused_computation.14 | convolution fusion | flops 1623195648 | bytes 18874560 | tf_op jit(solution)/shard_map/nij,njr->nir/dot_general | solution.py:32
  70.4 8.4 %fusion.6 = f32[16,256,128]{2,0,1:T(8,128)S(1)} fusion(f32[48,256,128]{2,1,0:T(8,128)} %fusion.10, s32[48]{0:T(128)S(1)} %copy-done.1), kind=kOutput, calls=%fused_computation.11 | convolution fusion | flops 301990656 | bytes 8388800 | tf_op jit(solution)/shard_map/bn,nir->bir/dot_general | solution.py:33
  78.8 2.0 copy.8
  80.8 0.0 all-reduce.3.cloned.1.call-update
  80.8 0.0 all-reduce.5.cloned.1.call-start
  80.9 31.9 %psum.29 = f32[128]{0:T(128)S(1)} all-reduce(f32[128]{0:T(128)S(1)} %get-tuple-element.5), channel_id=1, replica_groups=mesh['cell'=2,'gene'=16] {'gene'}, use_global_device_ids=true, to_apply=%region_2.0 | all-reduce | flops 128 | bytes 1024 | tf_op jit(solution)/shard_map/psum | solution.py:20
  112.8 65.2 %all-reduce.3.cloned.1.call-done = f32[4096,128]{1,0:T(8,128)} async-done(((f32[4096,128]{1,0:T(8,128)}), f32[4096,128]{1,0:T(8,128)}) %all-reduce.3.cloned.1.call-update) | async-done | bytes 2097168 | tf_op jit(solution)/shard_map/psum | solution.py:36
  177.9 2.8 %fusion.22 = (f32[128]{0:T(128)S(1)}, f32[4096,128]{1,0:T(8,128)S(1)}) fusion(f32[128]{0:T(128)S(1)} %psum.29, f32[4096,128]{1,0:T(8,128)} %all-gather.2.cloned.1.call-done, f32[4096,128]{1,0:T(8,128)} %all-reduce.3.cloned.1.call-done), kind=kLoop, calls=%fused_computation.31 | loop fusion | flops 1572736 | bytes 6292480 | tf_op jit(solution)/shard_map/reduce_sum | solution.py:39
  180.7 0.1 convert_element_type.33
  180.8 2.7 %gather_fusion.2 = bf16[48,256,128]{2,1,0:T(8,128)(2,1)} fusion(bf16[16,256,128]{2,1,0:T(8,128)(2,1)S(1)} %bitcast.20, s32[1024]{0:T(1024)S(1)} %pad_clamp_fusion.1), kind=kCustom, calls=%fused_computation.2 | custom fusion | bytes 6291648 | tf_op jit(solution)/shard_map/gather | solution.py:42
  183.5 0.0 copy-start.2
  183.5 12.2 %fusion.8 = f32[48,256,128]{2,1,0:T(8,128)} fusion(bf16[48,256,128]{2,1,0:T(8,128)(2,1)} %gather_fusion.2, bf16[48,256,256]{2,1,0:T(8,128)(2,1)} %param.6, f32[48]{0:T(128)S(1)} %compare_convert_fusion, bf16[48,256,128]{2,1,0:T(8,128)(2,1)} %gather_fusion.1), kind=kOutput, calls=%fused_computation.13 | convolution fusion | flops 1623195648 | bytes 18874560 | tf_op jit(solution)/shard_map/nij,nir->njr/dot_general | solution.py:44
  195.7 0.0 copy-done.2
  195.7 0.0 copy-start
  195.7 8.2 %fusion.4 = f32[4,256,128]{2,0,1:T(4,128)S(1)} fusion(f32[48,256,128]{2,1,0:T(8,128)} %fusion.8, s32[48]{0:T(128)S(1)} %copy-done.2), kind=kOutput, calls=%fused_computation.9 | convolution fusion | flops 75497664 | bytes 6815936 | tf_op jit(solution)/shard_map/bn,njr->bjr/dot_general | solution.py:47
  203.9 0.8 copy.9
  204.7 0.0 all-reduce.5.cloned.1.call-update
  204.7 4.9 %psum.31 = f32[128]{0:T(128)S(1)} all-reduce(f32[128]{0:T(128)S(1)} %get-tuple-element.2), channel_id=1, replica_groups=mesh['cell'=2,'gene'=16] {'cell'}, use_global_device_ids=true, to_apply=%region_5.0 | all-reduce | flops 128 | bytes 1024 | tf_op jit(solution)/shard_map/psum | solution.py:39
  209.7 0.7 constant_dynamic-slice_fusion
  210.3 22.5 %all-reduce.5.cloned.1.call-done = f32[1024,128]{1,0:T(8,128)} async-done(((f32[1024,128]{1,0:T(8,128)}), f32[1024,128]{1,0:T(8,128)}) %all-reduce.5.cloned.1.call-update) | async-done | bytes 524304 | tf_op jit(solution)/shard_map/psum | solution.py:50
  232.8 0.0 copy-done
  232.8 1.9 multiply_divide_fusion.1
  (4 shorter events, 0.0 us)
Async XLA Ops:
  7.2 47.2 %all-gather.2.cloned.1.call-start = ((), (), s32[]{:S(2)}) async-start(), calls=%async_computation | async-start | bytes 2228224 | tf_op jit(solution)/shard_map/all_gather | solution.py:21
  7.9 170.0 %all-reduce.3.cloned.1.call-start = ((), (), s32[]{:S(2)}) async-start(), calls=%async_computation.1 | async-start | bytes 4194304 | tf_op jit(solution)/shard_map/psum | solution.py:36
  10.7 2.8 %copy-start.1 = (s32[48]{0:T(128)S(1)}, s32[48]{0:T(128)}, u32[]{:S(2)}) copy-start(s32[48]{0:T(128)} %param.7) | copy-start | bytes 580
  80.8 152.0 %all-reduce.5.cloned.1.call-start = ((), (), s32[]{:S(2)}) async-start(), calls=%async_computation.2 | async-start | bytes 1048576 | tf_op jit(solution)/shard_map/psum | solution.py:50
  183.5 12.2 %copy-start.2 = (s32[48]{0:T(128)S(1)}, s32[48]{0:T(128)}, u32[]{:S(2)}) copy-start(s32[48]{0:T(128)} %param.8) | copy-start | bytes 580
  195.7 37.1 %copy-start = (f32[1024,128]{1,0:T(8,128)S(1)}, f32[1024,128]{1,0:T(8,128)}, u32[]{:S(2)}) copy-start(f32[1024,128]{1,0:T(8,128)} %param.11) | copy-start | bytes 1572868
Sparse Core Ops, SparseCore 0:
  10.1 44.1 all-gather.1
  80.9 96.9 all-reduce.2
  204.9 27.9 all-reduce.4
where the time goes:
time: 242 us; the launch traced here: 241 us
  waiting for transfers between devices  129 us (53%)
  matrix products  40.5 us (17%)
  blocking collectives  36.8 us (15%)
  between operations  14.4 us (6%)
  local copies, waits for them, and re-layouts  11.6 us (5%)
  other arithmetic  8.57 us (4%)
    psum x1, waiting for transfers between devices, on_device(): whole = lax.psum(numer, 'gene')  65.2 us
    all_gather x1, waiting for transfers between devices, on_device(): cell_full = lax.all_gather(cell_factor, 'gene', axis=0, tiled=True)  40.9 us
    psum x1, blocking collectives, on_device(): gene_totals = lax.psum(jnp.sum(gene_factor, 0), 'gene')  31.9 us
    psum x1, waiting for transfers between devices, on_device(): total = lax.psum(numer_gene, 'cell')  22.5 us
    dot_general x1, matrix products, on_device(): jnp.einsum('nij,nir->njr', ratio_next, new_tiles, preferred_element_type=...  12.2 us
    dot_general x1, matrix products, on_device(): jnp.einsum('nij,njr->nir', ratio, gene_tiles, preferred_element_type=jnp....  11.7 us
    dot_general x1, matrix products, on_device(): jnp.einsum('bn,nir->bir', row_pick, terms, precision=lax.Precision.HIGHEST)  8.37 us
    dot_general x1, matrix products, on_device(): jnp.einsum('bn,njr->bjr', col_pick, terms_next, precision=lax.Precision.H...  8.16 us
  transfers between devices with their start and end apart: 3, of which 3 were waited for; matrix products, arithmetic and copies ran while one was open for 2% of the time, Pallas kernels for 0%

commit v1 on v0

--- a/solution.py
+++ b/solution.py
@@ -33,7 +33,9 @@
     numer = jnp.einsum("bn,nir->bir", row_pick, terms, precision=lax.Precision.HIGHEST).reshape(
         -1, rank
     )
-    whole = lax.psum(numer, "gene")
+    whole = numer
+    for hop in (1, 2, 4, 8):
+        whole = whole + lax.ppermute(whole, "gene", [(dev, dev ^ hop) for dev in range(16)])
     group_new = cell_full * whole / gene_totals
     new_bf = group_new.astype(jnp.bfloat16)
     cell_sums = lax.psum(jnp.sum(group_new, 0), "cell")

time: 242 us -> 352 us (1.45)
  blocking collectives: 36.8 us -> 104 us
  waiting for transfers between devices: 129 us -> 171 us
    ppermute x0 -> x4, waiting for transfers between devices: none -> 97.7 us  [on_device(): lax.ppermute(whole, 'gene', [(dev, dev ^ hop) for dev in range(16)])]
    psum x1, blocking collectives: 31.9 us -> 98.9 us  [on_device(): gene_totals = lax.psum(jnp.sum(gene_factor, 0), 'gene')]
    psum x1 -> x0, waiting for transfers between devices: 65.2 us -> none  [on_device(): whole = lax.psum(numer, 'gene')]
    psum x1, waiting for transfers between devices: 22.5 us -> 31.3 us  [on_device(): total = lax.psum(numer_gene, 'cell')]
  transfers between devices with their start and end apart: 3 -> 6, of which waited for: 3 -> 5; matrix products, arithmetic and copies ran while one was open for 2% -> 2% of each run, Pallas kernels for 0% -> 0%
where the time goes in v1:
time: 352 us
  waiting for transfers between devices  171 us (49%)
  blocking collectives  104 us (30%)
  matrix products  40.5 us (12%)
  between operations  14.8 us (4%)
  local copies, waits for them, and re-layouts  10.3 us (3%)
  other arithmetic  9.85 us (3%)
    psum x1, blocking collectives, on_device(): gene_totals = lax.psum(jnp.sum(gene_factor, 0), 'gene')  98.9 us
    ppermute x4, waiting for transfers between devices, on_device(): lax.ppermute(whole, 'gene', [(dev, dev ^ hop) for dev in range(16)])  97.7 us
    all_gather x1, waiting for transfers between devices, on_device(): cell_full = lax.all_gather(cell_factor, 'gene', axis=0, tiled=True)  40.9 us
    psum x1, waiting for transfers between devices, on_device(): total = lax.psum(numer_gene, 'cell')  31.3 us
    dot_general x1, matrix products, on_device(): jnp.einsum('nij,nir->njr', ratio_next, new_tiles, preferred_element_type=...  12.2 us
    dot_general x1, matrix products, on_device(): jnp.einsum('nij,njr->nir', ratio, gene_tiles, preferred_element_type=jnp....  11.7 us
    dot_general x1, matrix products, on_device(): jnp.einsum('bn,nir->bir', row_pick, terms, precision=lax.Precision.HIGHEST)  8.37 us
    dot_general x1, matrix products, on_device(): jnp.einsum('bn,njr->bjr', col_pick, terms_next, precision=lax.Precision.H...  8.16 us
  transfers between devices with their start and end apart: 6, of which 5 were waited for; matrix products, arithmetic and copies ran while one was open for 2% of the time, Pallas kernels for 0%

profile of v1, /device:TPU:0, one launch (start us, length us, event | category | flops | bytes accessed | tf_op | source)
XLA Modules:
  0.0 352.0 jit_solution(16150226813427497031)
XLA Ops:
  7.2 0.0 all-gather.2.cloned.1.call-start
  7.2 0.7 all-gather.2.cloned.1.call-update
  7.9 0.0 all-reduce.2.cloned.1.call-start
  8.6 0.7 compare_select_fusion
  9.3 1.4 fusion.23
  10.7 0.0 copy-start.2
  10.7 2.7 gather_fusion.1
  13.4 0.0 copy-done.2
  13.4 40.9 %all-gather.2.cloned.1.call-done = f32[4096,128]{1,0:T(8,128)} async-done(((f32[256,128]{1,0:T(8,128)}), f32[4096,128]{1,0:T(8,128)}) %all-gather.2.cloned.1.call-update) | async-done | bytes 2097168 | tf_op jit(solution)/shard_map/all_gather | solution.py:21
  54.3 1.7 convert_element_type.29
  56.0 2.7 gather_fusion
  58.7 11.7 %fusion.10 = f32[48,256,128]{2,1,0:T(8,128)} fusion(bf16[48,256,128]{2,1,0:T(8,128)(2,1)} %gather_fusion.1, bf16[48,256,256]{2,1,0:T(8,128)(2,1)} %param.6, f32[48]{0:T(128)S(1)} %compare_convert_fusion, bf16[48,256,128]{2,1,0:T(8,128)(2,1)} %gather_fusion), kind=kOutput, calls=%fused_computation.14 | convolution fusion | flops 1623195648 | bytes 18874560 | tf_op jit(solution)/shard_map/nij,njr->nir/dot_general | solution.py:32
  70.4 8.4 %fusion.6 = f32[16,256,128]{2,0,1:T(8,128)S(1)} fusion(f32[48,256,128]{2,1,0:T(8,128)} %fusion.10, s32[48]{0:T(128)S(1)} %copy-done.2), kind=kOutput, calls=%fused_computation.11 | convolution fusion | flops 301990656 | bytes 8388800 | tf_op jit(solution)/shard_map/bn,nir->bir/dot_general | solution.py:33
  78.8 0.7 copy.8
  79.5 0.3 collective-permute-start
  79.8 3.9 %collective-permute-done = f32[4096,128]{1,0:T(8,128)S(1)} collective-permute-done((f32[4096,128]{1,0:T(8,128)S(1)}, f32[4096,128]{1,0:T(8,128)S(1)}, u32[]{:S(2)}, u32[]{:S(2)}) %collective-permute-start) | collective-permute-done | bytes 2097184 | tf_op jit(solution)/shard_map/ppermute | solution.py:38
  83.7 0.2 bitcast_add_fusion
  83.9 0.7 collective-permute-start.1
  84.6 47.2 %collective-permute-done.1 = f32[4096,128]{1,0:T(8,128)S(1)} collective-permute-done((f32[4096,128]{1,0:T(8,128)S(1)}, f32[4096,128]{1,0:T(8,128)S(1)}, u32[]{:S(2)}, u32[]{:S(2)}) %collective-permute-start.1) | collective-permute-done | bytes 2097184 | tf_op jit(solution)/shard_map/ppermute | solution.py:38
  131.8 0.2 add.35
  132.0 0.4 collective-permute-start.2
  132.4 46.6 %collective-permute-done.2 = f32[4096,128]{1,0:T(8,128)S(1)} collective-permute-done((f32[4096,128]{1,0:T(8,128)S(1)}, f32[4096,128]{1,0:T(8,128)S(1)}, u32[]{:S(2)}, u32[]{:S(2)}) %collective-permute-start.2) | collective-permute-done | bytes 2097184 | tf_op jit(solution)/shard_map/ppermute | solution.py:38
  178.9 0.2 add.36
  179.2 0.0 copy-start
  179.2 0.9 collective-permute-start.3
  180.1 98.9 %psum.21 = f32[128]{0:T(128)S(1)} all-reduce(f32[128]{0:T(128)S(1)} %get-tuple-element.5), channel_id=1, replica_groups=mesh['cell'=2,'gene'=16] {'gene'}, use_global_device_ids=true, to_apply=%region_1.0 | all-reduce | flops 128 | bytes 1024 | tf_op jit(solution)/shard_map/psum | solution.py:20
  279.0 0.0 copy-done
  279.0 0.0 collective-permute-done.3
  279.0 3.4 fusion.22
  282.4 0.1 convert_element_type.33
  282.5 2.7 gather_fusion.2
  285.2 0.0 copy-start.3
  285.2 12.2 %fusion.8 = f32[48,256,128]{2,1,0:T(8,128)} fusion(bf16[48,256,128]{2,1,0:T(8,128)(2,1)} %gather_fusion.2, bf16[48,256,256]{2,1,0:T(8,128)(2,1)} %param.6, f32[48]{0:T(128)S(1)} %compare_convert_fusion, bf16[48,256,128]{2,1,0:T(8,128)(2,1)} %gather_fusion.1), kind=kOutput, calls=%fused_computation.13 | convolution fusion | flops 1623195648 | bytes 18874560 | tf_op jit(solution)/shard_map/nij,nir->njr/dot_general | solution.py:46
  297.4 0.0 copy-done.3
  297.4 0.0 copy-start.1
  297.4 8.2 %fusion.4 = f32[4,256,128]{2,0,1:T(4,128)S(1)} fusion(f32[48,256,128]{2,1,0:T(8,128)} %fusion.8, s32[48]{0:T(128)S(1)} %copy-done.3), kind=kOutput, calls=%fused_computation.9 | convolution fusion | flops 75497664 | bytes 6815936 | tf_op jit(solution)/shard_map/bn,njr->bjr/dot_general | solution.py:49
  305.6 0.8 copy.9
  306.4 0.0 all-reduce.2.cloned.1.call-update
  306.5 4.9 %psum.23 = f32[128]{0:T(128)S(1)} all-reduce(f32[128]{0:T(128)S(1)} %get-tuple-element.2), channel_id=1, replica_groups=mesh['cell'=2,'gene'=16] {'cell'}, use_global_device_ids=true, to_apply=%region_4.0 | all-reduce | flops 128 | bytes 1024 | tf_op jit(solution)/shard_map/psum | solution.py:41
  311.4 0.7 constant_dynamic-slice_fusion
  312.1 31.3 %all-reduce.2.cloned.1.call-done = f32[1024,128]{1,0:T(8,128)} async-done(((f32[1024,128]{1,0:T(8,128)}), f32[1024,128]{1,0:T(8,128)}) %all-reduce.2.cloned.1.call-update) | async-done | bytes 524304 | tf_op jit(solution)/shard_map/psum | solution.py:52
  343.3 0.0 copy-done.1
  343.3 1.9 multiply_divide_fusion.1
  (4 shorter events, 0.0 us)
Async XLA Ops:
  7.2 47.2 %all-gather.2.cloned.1.call-start = ((), (), s32[]{:S(2)}) async-start(), calls=%async_computation | async-start | bytes 2228224 | tf_op jit(solution)/shard_map/all_gather | solution.py:21
  7.9 335.4 %all-reduce.2.cloned.1.call-start = ((), (), s32[]{:S(2)}) async-start(), calls=%async_computation.1 | async-start | bytes 1048576 | tf_op jit(solution)/shard_map/psum | solution.py:52
  10.7 2.8 copy-start.2
  79.5 4.2 %collective-permute-start = (f32[4096,128]{1,0:T(8,128)S(1)}, f32[4096,128]{1,0:T(8,128)S(1)}, u32[]{:S(2)}, u32[]{:S(2)}) collective-permute-start(f32[4096,128]{1,0:T(8,128)S(1)} %bitcast.23), channel_id=1, source_target_pairs={{0,1},{1,0},{2,3},{3,2},{4,5},{5,4},{6,7},{7,6},{8,9},{9,8},{10,11... | collective-permute-start | bytes 6291464 | tf_op jit(solution)/shard_map/ppermute | solution.py:38
  83.9 47.8 %collective-permute-start.1 = (f32[4096,128]{1,0:T(8,128)S(1)}, f32[4096,128]{1,0:T(8,128)S(1)}, u32[]{:S(2)}, u32[]{:S(2)}) collective-permute-start(f32[4096,128]{1,0:T(8,128)S(1)} %bitcast_add_fusion), channel_id=1, source_target_pairs={{0,2},{1,3},{2,0},{3,1},{4,6},{5,7},{6,4},{7,5},{8,10},{9,11},{10,... | collective-permute-start | bytes 6291464 | tf_op jit(solution)/shard_map/ppermute | solution.py:38
  132.0 47.0 %collective-permute-start.2 = (f32[4096,128]{1,0:T(8,128)S(1)}, f32[4096,128]{1,0:T(8,128)S(1)}, u32[]{:S(2)}, u32[]{:S(2)}) collective-permute-start(f32[4096,128]{1,0:T(8,128)S(1)} %add.35), channel_id=1, source_target_pairs={{0,4},{1,5},{2,6},{3,7},{4,0},{5,1},{6,2},{7,3},{8,12},{9,13},{10,... | collective-permute-start | bytes 6291464 | tf_op jit(solution)/shard_map/ppermute | solution.py:38
  179.2 99.8 %copy-start = (f32[4096,128]{1,0:T(8,128)}, f32[4096,128]{1,0:T(8,128)S(1)}, u32[]{:S(2)}) copy-start(f32[4096,128]{1,0:T(8,128)S(1)} %add.36) | copy-start | bytes 6291460
  179.2 99.8 %collective-permute-start.3 = (f32[4096,128]{1,0:T(8,128)S(1)}, f32[4096,128]{1,0:T(8,128)}, u32[]{:S(2)}, u32[]{:S(2)}) collective-permute-start(f32[4096,128]{1,0:T(8,128)S(1)} %add.36), channel_id=1, source_target_pairs={{0,8},{1,9},{2,10},{3,11},{4,12},{5,13},{6,14},{7,15},{8,0},{9,1},... | collective-permute-start | bytes 6291464 | tf_op jit(solution)/shard_map/ppermute | solution.py:38
  285.2 12.2 %copy-start.3 = (s32[48]{0:T(128)S(1)}, s32[48]{0:T(128)}, u32[]{:S(2)}) copy-start(s32[48]{0:T(128)} %param.8) | copy-start | bytes 580
  297.4 45.9 %copy-start.1 = (f32[1024,128]{1,0:T(8,128)S(1)}, f32[1024,128]{1,0:T(8,128)}, u32[]{:S(2)}) copy-start(f32[1024,128]{1,0:T(8,128)} %param.11) | copy-start | bytes 1572868
Sparse Core Ops, SparseCore 0:
  10.1 44.1 all-gather.1
  306.6 36.6 all-reduce.1
